TPU v7x, 128 devices: a whole 4x4x4 slice. The times are simulated.
128 devices in a mesh: seq: 32 (over x, y, core), head: 4 (over z).
Axes of the slice: x: 4, y: 4, z: 4, core: 2. Of those that a mesh axis runs over, the one named last changes fastest.
Arguments:
- group_of: int32 [32], replicated, may hold values from 0 to 31, as said below
- soft_query: bfloat16 [8192, 1536], P('seq', 'head'), may hold values from -8 to 8
- soft_key: bfloat16 [8192, 1536], P('seq', 'head'), may hold values from -8 to 8
- soft_value: bfloat16 [8192, 1536], P('seq', 'head'), may hold values from -6 to 6
- soft_grad: bfloat16 [8192, 1536], P('seq', 'head'), may hold values from -6 to 6
- lin_query: bfloat16 [8192, 1536], P('seq', 'head'), may hold values from -6 to 6
- lin_key: bfloat16 [8192, 1536], P('seq', 'head'), may hold values from -0.59765625 to 0.59765625
- lin_value: bfloat16 [8192, 1536], P('seq', 'head'), may hold values from -40 to 40
- log_decay: float32 [8192, 12], P('seq', 'head'), may hold values from -1 to 0
- lin_grad: bfloat16 [8192, 1536], P('seq', 'head'), may hold values from -6 to 6
Outputs:
- soft_out: bfloat16 [8192, 1536], P('seq', 'head')
- soft_dq: bfloat16 [8192, 1536], P('seq', 'head')
- soft_dk: bfloat16 [8192, 1536], P('seq', 'head')
- soft_dv: bfloat16 [8192, 1536], P('seq', 'head')
- lin_out: float32 [8192, 1536], P('seq', 'head')
- lin_dq: float32 [8192, 1536], P('seq', 'head')
- lin_dk: float32 [8192, 1536], P('seq', 'head')
- lin_dv: float32 [8192, 1536], P('seq', 'head')
Inputs may be any that keep to these rules, and one draw needn't show every extreme that they name: group_of[d] = (group_of[0] + d) mod 32: the indices of seq hold the sequence's blocks in order around the axis, from a drawn first index.
All inputs are finite; a program needn't handle non-finite values.
Results may differ from a plain program's by a relative error of at most 0.017.
Values may be sent and summed in bfloat16 or wider, within the bound.
No kernel may reach another device: no remote copies, remote signals or barrier semaphores. Data moves between devices by JAX's collectives and lax.ppermute only.
A program may use at most 128 MiB of HBM per device.

v0:
```python
import jax
import jax.numpy as jnp
from jax import lax
from jax.sharding import PartitionSpec as P

HEAD_TOTAL = 12
HEAD_DIM = 128
EPS = 1e-06
HIGHEST = lax.Precision.HIGHEST


def shifted(block, axis, distance):
    devices = range(lax.axis_size(axis))
    route = [((i - distance) % len(devices), i) for i in devices]
    return lax.ppermute(block, axis, route)


def shortened(x):
    return jax.tree.map(lambda a: a.astype(jnp.bfloat16) if a.dtype == jnp.float32 else a, x)


def split_heads(matrix):
    return matrix.reshape(matrix.shape[0], matrix.shape[1] // HEAD_DIM, HEAD_DIM)


def chain_weights(device_groups, own_group, group_logs, forward):
    if forward:
        source_mask = device_groups < own_group
        between = (device_groups[:, None] < device_groups[None, :]) & (
            device_groups[None, :] < own_group
        )
    else:
        source_mask = device_groups > own_group
        between = (device_groups[:, None] > device_groups[None, :]) & (
            device_groups[None, :] > own_group
        )
    exponent = jnp.dot(between.astype(jnp.float32), group_logs, precision=HIGHEST)
    return jnp.where(source_mask[:, None], jnp.exp(exponent), 0.0)


def on_device(
    group_of,
    soft_query,
    soft_key,
    soft_value,
    soft_grad,
    lin_query,
    lin_key,
    lin_value,
    log_decay,
    lin_grad,
):
    tok_rows = soft_query.shape[0]
    feat_width = soft_query.shape[1]
    heads_here = feat_width // HEAD_DIM
    seq_count = lax.axis_size("seq")
    score_scale = HEAD_DIM ** (-0.5)
    own_group = group_of[lax.axis_index("seq")]
    row_index = jnp.arange(tok_rows, dtype=jnp.int32)
    query_pos = own_group * tok_rows + row_index
    block_keys = min(512, seq_count * tok_rows)
    keys_all, values_all = (
        lax.all_gather(soft_key, "seq", axis=0, tiled=True),
        lax.all_gather(soft_value, "seq", axis=0, tiled=True),
    )
    keys_all = jnp.roll(keys_all, group_of[0] * tok_rows, axis=0)
    values_all = jnp.roll(values_all, group_of[0] * tok_rows, axis=0)
    block_count = (query_pos[-1] + block_keys) // block_keys
    queries = split_heads(soft_query)
    grad_heads = split_heads(soft_grad)

    def key_block(block_index):
        block_start = block_index * block_keys
        key_part = split_heads(lax.dynamic_slice_in_dim(keys_all, block_start, block_keys, 0))
        value_part = split_heads(lax.dynamic_slice_in_dim(values_all, block_start, block_keys, 0))
        key_pos = block_start + jnp.arange(block_keys, dtype=jnp.int32)
        scores = (
            jnp.einsum("thd,khd->htk", queries, key_part, preferred_element_type=jnp.float32)
            * score_scale
        )
        keep_mask = key_pos[None, :] <= query_pos[:, None]
        return (jnp.where(keep_mask[None], scores, -jnp.inf), key_part, value_part)

    def max_sum(block_index, carry):
        old_max, exp_total = carry
        scores = key_block(block_index)[0]
        updated_maximum = jnp.maximum(old_max, jnp.max(scores, axis=2))
        exp_total = exp_total * jnp.exp(old_max - updated_maximum) + jnp.sum(
            jnp.exp(scores - updated_maximum[:, :, None]), axis=2
        )
        return (updated_maximum, exp_total)

    start_max = jnp.full((heads_here, tok_rows), -jnp.inf, jnp.float32)
    start_total = jnp.zeros((heads_here, tok_rows), jnp.float32)
    row_max, exp_total = lax.fori_loop(0, block_count, max_sum, (start_max, start_total))
    log_total = row_max + jnp.log(exp_total)

    def out_step(block_index, out_sum):
        scores, key_part, value_part = key_block(block_index)
        probs_half = jnp.exp(scores - log_total[:, :, None]).astype(jnp.bfloat16)
        return out_sum + jnp.einsum(
            "htk,khd->thd", probs_half, value_part, preferred_element_type=jnp.float32
        )

    head_zeros = jnp.zeros((tok_rows, heads_here, HEAD_DIM), jnp.float32)
    soft_out = (
        lax.fori_loop(0, block_count, out_step, head_zeros)
        .reshape(tok_rows, feat_width)
        .astype(jnp.bfloat16)
    )
    delta_rows = jnp.sum(
        grad_heads.astype(jnp.float32) * split_heads(soft_out).astype(jnp.float32), axis=2
    ).T
    own_keys = split_heads(soft_key)
    own_values = split_heads(soft_value)

    def key_side(shift_count, cycle_state):

        def work(cycle_state):
            key_sums, cycle_parts = cycle_state
            query_part = split_heads(cycle_parts[0])
            grad_part = split_heads(cycle_parts[1])
            scores = (
                jnp.einsum("thd,khd->htk", query_part, own_keys, preferred_element_type=jnp.float32)
                * score_scale
            )
            keep_mask = row_index[None, :] <= row_index[:, None] + shift_count * tok_rows
            probs_full = jnp.exp(
                jnp.where(keep_mask[None], scores - cycle_parts[2][:, :, None], -jnp.inf)
            )
            probs_half = probs_full.astype(jnp.bfloat16)
            dprobs = jnp.einsum(
                "thd,khd->htk", grad_part, own_values, preferred_element_type=jnp.float32
            )
            dscores = (probs_full * (dprobs - cycle_parts[3][:, :, None])).astype(jnp.bfloat16)
            key_grad = key_sums[0] + jnp.einsum(
                "htk,thd->khd", dscores, query_part, preferred_element_type=jnp.float32
            )
            value_grad = key_sums[1] + jnp.einsum(
                "htk,thd->khd", probs_half, grad_part, preferred_element_type=jnp.float32
            )
            return ((key_grad, value_grad), cycle_parts)

        return lax.cond(
            own_group + shift_count < seq_count, work, lambda cycle_state: cycle_state, cycle_state
        )

    def cycle_step(shift_count, cycle_state):
        key_sums, cycle_parts = key_side(shift_count, cycle_state)
        cycle_parts = shifted(cycle_parts, "seq", -1)
        return (key_sums, cycle_parts)

    cycle_parts = (soft_query, soft_grad, log_total, delta_rows)
    cycle_state = lax.fori_loop(
        0, seq_count - 1, cycle_step, ((head_zeros, head_zeros), cycle_parts)
    )
    (key_grad, value_grad), cycle_parts = key_side(seq_count - 1, cycle_state)

    def dq_step(block_index, grad_sum):
        scores, key_part, value_part = key_block(block_index)
        probs_full = jnp.exp(scores - log_total[:, :, None])
        dprobs = jnp.einsum(
            "thd,khd->htk", grad_heads, value_part, preferred_element_type=jnp.float32
        )
        dscores = (probs_full * (dprobs - delta_rows[:, :, None])).astype(jnp.bfloat16)
        return grad_sum + jnp.einsum(
            "htk,khd->thd", dscores, key_part, preferred_element_type=jnp.float32
        )

    query_grad = lax.fori_loop(0, block_count, dq_step, head_zeros).reshape(tok_rows, feat_width)
    soft_dq = (query_grad * score_scale).astype(jnp.bfloat16)
    soft_dk = (key_grad * score_scale).reshape(tok_rows, feat_width).astype(jnp.bfloat16)
    soft_dv = value_grad.reshape(tok_rows, feat_width).astype(jnp.bfloat16)

    def heads_first(matrix):
        return split_heads(matrix).astype(jnp.float32).transpose(1, 0, 2)

    def rows_first(stacked):
        return stacked.transpose(1, 0, 2).reshape(tok_rows, feat_width)

    lin_queries = heads_first(lin_query)
    lin_keys = heads_first(lin_key)
    lin_values = heads_first(lin_value)
    cumulative = jnp.cumsum(log_decay, axis=0).T
    group_log = cumulative[:, -1]
    lower_mask = (row_index[:, None] >= row_index[None, :])[None]
    log_gap = cumulative[:, :, None] - cumulative[:, None, :]
    inner_decay = jnp.where(lower_mask, jnp.exp(jnp.where(lower_mask, log_gap, 0.0)), 0.0)
    inner_scores = (
        jnp.einsum("htd,hsd->hts", lin_queries, lin_keys, precision=HIGHEST) * inner_decay
    )
    local_out = jnp.einsum("hts,hsd->htd", inner_scores, lin_values, precision=HIGHEST)
    tail_decay = jnp.exp(group_log[:, None] - cumulative)
    head_decay = jnp.exp(cumulative)
    local_state = jnp.einsum(
        "hsd,hse->hde", lin_keys * tail_decay[:, :, None], lin_values, precision=HIGHEST
    )
    flat_state = local_state.reshape(heads_here, HEAD_DIM * HEAD_DIM)
    states_all, logs_all = (
        lax.all_gather(flat_state[None].astype(jnp.bfloat16), "seq", axis=0, tiled=True).astype(
            jnp.float32
        ),
        lax.all_gather(group_log[None].astype(jnp.bfloat16), "seq", axis=0, tiled=True).astype(
            jnp.float32
        ),
    )
    weight = chain_weights(group_of, own_group, logs_all, True)
    entry_state = jnp.einsum("jh,jhx->hx", weight, states_all, precision=HIGHEST)
    entry_mat = entry_state.reshape(heads_here, HEAD_DIM, HEAD_DIM)
    raw_out = local_out + head_decay[:, :, None] * jnp.einsum(
        "htd,hde->hte", lin_queries, entry_mat, precision=HIGHEST
    )
    raw_rows = rows_first(raw_out)
    square_sum = lax.psum(jnp.sum(raw_rows * raw_rows, axis=1), "head")
    row_rms = jnp.sqrt(square_sum / (HEAD_TOTAL * HEAD_DIM) + EPS)
    lin_out = raw_rows / row_rms[:, None]
    upstream = lin_grad.astype(jnp.float32)
    aligned = lax.psum(jnp.sum(upstream * lin_out, axis=1), "head")
    raw_grad_rows = (upstream - lin_out * (aligned / (HEAD_TOTAL * HEAD_DIM))[:, None]) / row_rms[
        :, None
    ]
    raw_grad = raw_grad_rows.reshape(tok_rows, heads_here, HEAD_DIM).transpose(1, 0, 2)
    value_local = jnp.einsum("hts,htd->hsd", inner_scores, raw_grad, precision=HIGHEST)
    inner_grad = jnp.einsum("htd,hsd->hts", raw_grad, lin_values, precision=HIGHEST) * inner_decay
    query_lin = jnp.einsum("hts,hsd->htd", inner_grad, lin_keys, precision=HIGHEST)
    query_lin = query_lin + head_decay[:, :, None] * jnp.einsum(
        "hte,hde->htd", raw_grad, entry_mat, precision=HIGHEST
    )
    key_local = jnp.einsum("hts,htd->hsd", inner_grad, lin_queries, precision=HIGHEST)
    read_grad = jnp.einsum(
        "htd,hte->hde", lin_queries * head_decay[:, :, None], raw_grad, precision=HIGHEST
    )
    read_grad = read_grad.reshape(heads_here, HEAD_DIM * HEAD_DIM)
    grads_all = lax.all_gather(shortened(read_grad[None]), "seq", axis=0, tiled=True)
    weight_back = chain_weights(group_of, own_group, logs_all, False)
    exit_grad = jnp.einsum("jh,jhx->hx", weight_back, grads_all, precision=HIGHEST)
    exit_mat = exit_grad.reshape(heads_here, HEAD_DIM, HEAD_DIM)
    lin_dk = key_local + tail_decay[:, :, None] * jnp.einsum(
        "hde,hse->hsd", exit_mat, lin_values, precision=HIGHEST
    )
    lin_dv = value_local + tail_decay[:, :, None] * jnp.einsum(
        "hde,hsd->hse", exit_mat, lin_keys, precision=HIGHEST
    )
    return (
        soft_out,
        soft_dq,
        soft_dk,
        soft_dv,
        lin_out,
        rows_first(query_lin),
        rows_first(lin_dk),
        rows_first(lin_dv),
    )


def solution(mesh):
    placed = (
        P(),
        P("seq", "head"),
        P("seq", "head"),
        P("seq", "head"),
        P("seq", "head"),
        P("seq", "head"),
        P("seq", "head"),
        P("seq", "head"),
        P("seq", "head"),
        P("seq", "head"),
    )
    return jax.shard_map(
        on_device,
        mesh=mesh,
        in_specs=placed,
        out_specs=(
            P("seq", "head"),
            P("seq", "head"),
            P("seq", "head"),
            P("seq", "head"),
            P("seq", "head"),
            P("seq", "head"),
            P("seq", "head"),
            P("seq", "head"),
        ),
        check_vma=False,
    )
```

profile of v0, /device:TPU:1, one launch (start us, length us, event | category | flops | bytes accessed | tf_op | source)
XLA Modules:
  0.0 711.8 jit_solution(17842653152815988040)
XLA Ops:
  16.7 63.9 %all-reduce = bf16[96]{0:T(256)(128)(2,1)S(1)} all-reduce(bf16[96]{0:T(256)(128)(2,1)S(1)} %dynamic-update-slice), channel_id=2, replica_groups=mesh['seq'=32,'head'=4] {'seq'}, use_global_device_ids=true, to_apply=%add | all-reduce | flops 96 | bytes 384
  84.9 6.8 fusion.60
  92.9 10.4 %psum.14 = f32[256]{0:T(256)S(1)} all-reduce(f32[256]{0:T(256)S(1)} %get-tuple-element.845), channel_id=1, replica_groups=mesh['seq'=32,'head'=4] {'head'}, use_global_device_ids=true, to_apply=%region_18.20 | all-reduce | flops 256 | bytes 2048 | tf_op jit(solution)/shard_map/psum | solution.py:214
  103.4 6.8 psum.15
  122.8 8.4 %fusion.56 = bf16[8192,384]{0,1:T(8,128)(2,1)} fusion(s32[]{:T(128)S(6)} %select_n.73, bf16[8192,384]{0,1:T(8,128)(2,1)} %all-gather.8.cloned.1.call-done), kind=kLoop, calls=%fused_computation.86 | loop fusion | flops 12582912 | bytes 12582916 | tf_op jit(solution)/shard_map/jit(_roll_dynamic)/concatenate | solution.py:66
  131.2 18.1 %while.60 = (s32[]{:T(128)}, f32[3,256]{1,0:T(4,128)S(1)}, f32[3,256]{1,0:T(4,128)S(1)}, s32[]{:T(128)}, bf16[8192,384]{0,1:T(8,128)(2,1)}, /*index=5*/bf16[256,...) while((s32[]{:T(128)}, f32[3,256]{1,0:T(4,128)S(1)}, ...), condition=%wide.region_3.5_spmd.clone, body=%wide.region_0.4_spmd.clone.sunk | while | flops 102762760 | bytes 4830375 | solution.py:95
  149.3 16.6 %all-gather.12.cloned.1.call-done = bf16[32,3,16384]{2,1,0:T(4,128)(2,1)} async-done(((bf16[1,3,16384]{2,1,0:T(4,128)(2,1)}), bf16[32,3,16384]{2,1,0:T(4,128)(2,1)}) %all-gather.12.cloned.1.call-update) | async-done | bytes 3145744 | tf_op jit(solution)/shard_map/all_gather | solution.py:234
  165.9 6.6 fusion.58
  174.8 46.7 %all-gather.6.cloned.1.call-done = bf16[8192,384]{0,1:T(8,128)(2,1)} async-done(((bf16[256,384]{0,1:T(8,128)(2,1)}), bf16[8192,384]{0,1:T(8,128)(2,1)}) %all-gather.6.cloned.1.call-update) | async-done | bytes 6291472 | tf_op jit(solution)/shard_map/all_gather | solution.py:64
  221.4 8.4 %fusion.57 = bf16[8192,384]{0,1:T(8,128)(2,1)} fusion(s32[]{:T(128)S(6)} %select_n.73, bf16[8192,384]{0,1:T(8,128)(2,1)} %all-gather.6.cloned.1.call-done), kind=kLoop, calls=%fused_computation.87 | loop fusion | flops 12582912 | bytes 12582916 | tf_op jit(solution)/shard_map/jit(_roll_dynamic)/concatenate | solution.py:67
  229.9 19.5 %while.61 = (s32[]{:T(128)}, f32[256,3,128]{0,2,1:T(8,128)S(1)}, s32[]{:T(128)}, bf16[8192,384]{0,1:T(8,128)(2,1)}, bf16[8192,384]{0,1:T(8,128)(2,1)}, /*index=5...) while((s32[]{:T(128)}, f32[256,3,128]{0,2,1:T(8,128)S(1)}, ...), condition=%wide.region_5.7_spmd.clone, body=%wide.region_4.6_spmd.clone.sunk | while | flops 203129600 | bytes 3613871 | solution.py:107
  251.0 46.1 %while.62 = (s32[]{:T(128)}, f32[256,3,128]{0,2,1:T(8,128)}, s32[]{:T(128)}, bf16[8192,384]{0,1:T(8,128)(2,1)}, bf16[256,3,128]{2,0,1:T(8,128)(2,1)S(1)}, /*inde...) while((s32[]{:T(128)}, f32[256,3,128]{0,2,1:T(8,128)}, ...), condition=%wide.region_8.10_spmd.clone, body=%wide.region_7.9_spmd.clone.sunk | while | flops 304579328 | bytes 7352511 | solution.py:170
  299.0 400.4 %while.63 = (s32[]{:T(128)}, f32[256,3,128]{2,0,1:T(8,128)S(1)}, f32[256,3,128]{2,0,1:T(8,128)S(1)}, bf16[256,384]{0,1:T(8,128)(2,1)S(1)}, bf16[256,384]{0,1:T(8...) while((s32[]{:T(128)}, f32[256,3,128]{2,0,1:T(8,128)S(1)}, ...), condition=%wide.region_12.14_spmd.clone.clone, body=%wide.region_9.13_spmd.clone.clone.sunk | while | flops 202965248 | bytes 7650759 | solution.py:154
  306.9 6.8 collective-permute-done.2
  325.5 4.4 conditional.6
  342.9 52.9 %collective-permute-start.1 = (bf16[256,384]{0,1:T(8,128)(2,1)}, bf16[256,384]{0,1:T(8,128)(2,1)S(1)}, u32[]{:S(2)}, u32[]{:S(2)}) collective-permute-start(bf16[256,384]{0,1:T(8,128)(2,1)} %copy.369), channel_id=1, source_target_pairs={{4,0},{8,4},{12,8},{16,12},{20,16},{24,20},{28,24},{32,28},{36,32}... | collective-permute-start | bytes 589832 | tf_op jit(solution)/shard_map/while/body/eval_jaxpr/ppermute | solution.py:15
  420.6 4.4 conditional.6
  489.7 4.4 conditional.6
  540.2 5.2 collective-permute-start.1
  551.7 5.2 collective-permute-start.1
  563.2 5.2 collective-permute-start.1
  574.7 5.2 collective-permute-start.1
  586.2 5.2 collective-permute-start.1
  597.7 5.2 collective-permute-start.1
  609.2 5.2 collective-permute-start.1
  620.7 5.2 collective-permute-start.1
  632.2 5.2 collective-permute-start.1
  643.8 5.2 collective-permute-start.1
  655.3 5.2 collective-permute-start.1
  666.8 5.2 collective-permute-start.1
  678.3 5.2 collective-permute-start.1
  689.8 5.2 collective-permute-start.1
  (788 shorter events, 418.8 us)
Async XLA Ops:
  7.2 77.7 %all-gather.10.cloned.1.call-start = ((), (), s32[]{:S(2)}) async-start(), calls=%async_computation.2 | async-start | bytes 4325376 | tf_op jit(solution)/shard_map/all_gather | solution.py:200
  12.7 110.1 %all-gather.8.cloned.1.call-start = ((), (), s32[]{:S(2)}) async-start(), calls=%async_computation.1 | async-start | bytes 6488064 | tf_op jit(solution)/shard_map/all_gather | solution.py:63
  14.5 151.4 %all-gather.12.cloned.1.call-start = ((), (), s32[]{:S(2)}) async-start(), calls=%async_computation.3 | async-start | bytes 4325376 | tf_op jit(solution)/shard_map/all_gather | solution.py:234
  111.5 109.9 %all-gather.6.cloned.1.call-start = ((), (), s32[]{:S(2)}) async-start(), calls=%async_computation | async-start | bytes 6488064 | tf_op jit(solution)/shard_map/all_gather | solution.py:64
  299.7 14.1 %collective-permute-start = (bf16[256,384]{0,1:T(8,128)(2,1)}, bf16[256,384]{0,1:T(8,128)(2,1)S(1)}, u32[]{:S(2)}, u32[]{:S(2)}) collective-permute-start(bf16[256,384]{0,1:T(8,128)(2,1)} %copy.368), channel_id=1, source_target_pairs={{4,0},{8,4},{12,8},{16,12},{20,16},{24,20},{28,24},{32,28},{36,32}... | collective-permute-start | bytes 589832 | tf_op jit(solution)/shard_map/while/body/eval_jaxpr/ppermute | solution.py:15
  300.6 13.2 %collective-permute-start.1 = (bf16[256,384]{0,1:T(8,128)(2,1)}, bf16[256,384]{0,1:T(8,128)(2,1)S(1)}, u32[]{:S(2)}, u32[]{:S(2)}) collective-permute-start(bf16[256,384]{0,1:T(8,128)(2,1)} %copy.369), channel_id=1, source_target_pairs={{4,0},{8,4},{12,8},{16,12},{20,16},{24,20},{28,24},{32,28},{36,32}... | collective-permute-start | bytes 589832 | tf_op jit(solution)/shard_map/while/body/eval_jaxpr/ppermute | solution.py:15
  301.2 12.5 %collective-permute-start.2 = (f32[3,256]{1,0:T(4,128)}, f32[3,256]{1,0:T(4,128)S(1)}, u32[]{:S(2)}, u32[]{:S(2)}) collective-permute-start(f32[3,256]{1,0:T(4,128)} %copy.370), channel_id=1, source_target_pairs={{4,0},{8,4},{12,8},{16,12},{20,16},{24,20},{28,24},{32,28},{36,32}... | collective-permute-start | bytes 9224 | tf_op jit(solution)/shard_map/while/body/eval_jaxpr/ppermute | solution.py:15
  301.8 11.9 %collective-permute-start.3 = (f32[3,256]{1,0:T(4,128)}, f32[3,256]{1,0:T(4,128)S(1)}, u32[]{:S(2)}, u32[]{:S(2)}) collective-permute-start(f32[3,256]{1,0:T(4,128)} %copy.371), channel_id=1, source_target_pairs={{4,0},{8,4},{12,8},{16,12},{20,16},{24,20},{28,24},{32,28},{36,32}... | collective-permute-start | bytes 9224 | tf_op jit(solution)/shard_map/while/body/eval_jaxpr/ppermute | solution.py:15
  342.2 60.2 %collective-permute-start = (bf16[256,384]{0,1:T(8,128)(2,1)}, bf16[256,384]{0,1:T(8,128)(2,1)S(1)}, u32[]{:S(2)}, u32[]{:S(2)}) collective-permute-start(bf16[256,384]{0,1:T(8,128)(2,1)} %copy.368), channel_id=1, source_target_pairs={{4,0},{8,4},{12,8},{16,12},{20,16},{24,20},{28,24},{32,28},{36,32}... | collective-permute-start | bytes 589832 | tf_op jit(solution)/shard_map/while/body/eval_jaxpr/ppermute | solution.py:15
  342.9 59.5 %collective-permute-start.1 = (bf16[256,384]{0,1:T(8,128)(2,1)}, bf16[256,384]{0,1:T(8,128)(2,1)S(1)}, u32[]{:S(2)}, u32[]{:S(2)}) collective-permute-start(bf16[256,384]{0,1:T(8,128)(2,1)} %copy.369), channel_id=1, source_target_pairs={{4,0},{8,4},{12,8},{16,12},{20,16},{24,20},{28,24},{32,28},{36,32}... | collective-permute-start | bytes 589832 | tf_op jit(solution)/shard_map/while/body/eval_jaxpr/ppermute | solution.py:15
  414.3 10.8 %collective-permute-start = (bf16[256,384]{0,1:T(8,128)(2,1)}, bf16[256,384]{0,1:T(8,128)(2,1)S(1)}, u32[]{:S(2)}, u32[]{:S(2)}) collective-permute-start(bf16[256,384]{0,1:T(8,128)(2,1)} %copy.368), channel_id=1, source_target_pairs={{4,0},{8,4},{12,8},{16,12},{20,16},{24,20},{28,24},{32,28},{36,32}... | collective-permute-start | bytes 589832 | tf_op jit(solution)/shard_map/while/body/eval_jaxpr/ppermute | solution.py:15
  425.8 10.8 %collective-permute-start = (bf16[256,384]{0,1:T(8,128)(2,1)}, bf16[256,384]{0,1:T(8,128)(2,1)S(1)}, u32[]{:S(2)}, u32[]{:S(2)}) collective-permute-start(bf16[256,384]{0,1:T(8,128)(2,1)} %copy.368), channel_id=1, source_target_pairs={{4,0},{8,4},{12,8},{16,12},{20,16},{24,20},{28,24},{32,28},{36,32}... | collective-permute-start | bytes 589832 | tf_op jit(solution)/shard_map/while/body/eval_jaxpr/ppermute | solution.py:15
  437.3 10.8 %collective-permute-start = (bf16[256,384]{0,1:T(8,128)(2,1)}, bf16[256,384]{0,1:T(8,128)(2,1)S(1)}, u32[]{:S(2)}, u32[]{:S(2)}) collective-permute-start(bf16[256,384]{0,1:T(8,128)(2,1)} %copy.368), channel_id=1, source_target_pairs={{4,0},{8,4},{12,8},{16,12},{20,16},{24,20},{28,24},{32,28},{36,32}... | collective-permute-start | bytes 589832 | tf_op jit(solution)/shard_map/while/body/eval_jaxpr/ppermute | solution.py:15
  448.9 10.8 %collective-permute-start = (bf16[256,384]{0,1:T(8,128)(2,1)}, bf16[256,384]{0,1:T(8,128)(2,1)S(1)}, u32[]{:S(2)}, u32[]{:S(2)}) collective-permute-start(bf16[256,384]{0,1:T(8,128)(2,1)} %copy.368), channel_id=1, source_target_pairs={{4,0},{8,4},{12,8},{16,12},{20,16},{24,20},{28,24},{32,28},{36,32}... | collective-permute-start | bytes 589832 | tf_op jit(solution)/shard_map/while/body/eval_jaxpr/ppermute | solution.py:15
  471.9 10.8 %collective-permute-start = (bf16[256,384]{0,1:T(8,128)(2,1)}, bf16[256,384]{0,1:T(8,128)(2,1)S(1)}, u32[]{:S(2)}, u32[]{:S(2)}) collective-permute-start(bf16[256,384]{0,1:T(8,128)(2,1)} %copy.368), channel_id=1, source_target_pairs={{4,0},{8,4},{12,8},{16,12},{20,16},{24,20},{28,24},{32,28},{36,32}... | collective-permute-start | bytes 589832 | tf_op jit(solution)/shard_map/while/body/eval_jaxpr/ppermute | solution.py:15
  483.4 10.8 %collective-permute-start = (bf16[256,384]{0,1:T(8,128)(2,1)}, bf16[256,384]{0,1:T(8,128)(2,1)S(1)}, u32[]{:S(2)}, u32[]{:S(2)}) collective-permute-start(bf16[256,384]{0,1:T(8,128)(2,1)} %copy.368), channel_id=1, source_target_pairs={{4,0},{8,4},{12,8},{16,12},{20,16},{24,20},{28,24},{32,28},{36,32}... | collective-permute-start | bytes 589832 | tf_op jit(solution)/shard_map/while/body/eval_jaxpr/ppermute | solution.py:15
  506.4 10.8 %collective-permute-start = (bf16[256,384]{0,1:T(8,128)(2,1)}, bf16[256,384]{0,1:T(8,128)(2,1)S(1)}, u32[]{:S(2)}, u32[]{:S(2)}) collective-permute-start(bf16[256,384]{0,1:T(8,128)(2,1)} %copy.368), channel_id=1, source_target_pairs={{4,0},{8,4},{12,8},{16,12},{20,16},{24,20},{28,24},{32,28},{36,32}... | collective-permute-start | bytes 589832 | tf_op jit(solution)/shard_map/while/body/eval_jaxpr/ppermute | solution.py:15
  527.5 10.8 %collective-permute-start = (bf16[256,384]{0,1:T(8,128)(2,1)}, bf16[256,384]{0,1:T(8,128)(2,1)S(1)}, u32[]{:S(2)}, u32[]{:S(2)}) collective-permute-start(bf16[256,384]{0,1:T(8,128)(2,1)} %copy.368), channel_id=1, source_target_pairs={{4,0},{8,4},{12,8},{16,12},{20,16},{24,20},{28,24},{32,28},{36,32}... | collective-permute-start | bytes 589832 | tf_op jit(solution)/shard_map/while/body/eval_jaxpr/ppermute | solution.py:15
  539.0 10.8 %collective-permute-start = (bf16[256,384]{0,1:T(8,128)(2,1)}, bf16[256,384]{0,1:T(8,128)(2,1)S(1)}, u32[]{:S(2)}, u32[]{:S(2)}) collective-permute-start(bf16[256,384]{0,1:T(8,128)(2,1)} %copy.368), channel_id=1, source_target_pairs={{4,0},{8,4},{12,8},{16,12},{20,16},{24,20},{28,24},{32,28},{36,32}... | collective-permute-start | bytes 589832 | tf_op jit(solution)/shard_map/while/body/eval_jaxpr/ppermute | solution.py:15
  550.5 10.8 %collective-permute-start = (bf16[256,384]{0,1:T(8,128)(2,1)}, bf16[256,384]{0,1:T(8,128)(2,1)S(1)}, u32[]{:S(2)}, u32[]{:S(2)}) collective-permute-start(bf16[256,384]{0,1:T(8,128)(2,1)} %copy.368), channel_id=1, source_target_pairs={{4,0},{8,4},{12,8},{16,12},{20,16},{24,20},{28,24},{32,28},{36,32}... | collective-permute-start | bytes 589832 | tf_op jit(solution)/shard_map/while/body/eval_jaxpr/ppermute | solution.py:15
  562.0 10.8 %collective-permute-start = (bf16[256,384]{0,1:T(8,128)(2,1)}, bf16[256,384]{0,1:T(8,128)(2,1)S(1)}, u32[]{:S(2)}, u32[]{:S(2)}) collective-permute-start(bf16[256,384]{0,1:T(8,128)(2,1)} %copy.368), channel_id=1, source_target_pairs={{4,0},{8,4},{12,8},{16,12},{20,16},{24,20},{28,24},{32,28},{36,32}... | collective-permute-start | bytes 589832 | tf_op jit(solution)/shard_map/while/body/eval_jaxpr/ppermute | solution.py:15
  573.5 10.8 %collective-permute-start = (bf16[256,384]{0,1:T(8,128)(2,1)}, bf16[256,384]{0,1:T(8,128)(2,1)S(1)}, u32[]{:S(2)}, u32[]{:S(2)}) collective-permute-start(bf16[256,384]{0,1:T(8,128)(2,1)} %copy.368), channel_id=1, source_target_pairs={{4,0},{8,4},{12,8},{16,12},{20,16},{24,20},{28,24},{32,28},{36,32}... | collective-permute-start | bytes 589832 | tf_op jit(solution)/shard_map/while/body/eval_jaxpr/ppermute | solution.py:15
  585.0 10.8 %collective-permute-start = (bf16[256,384]{0,1:T(8,128)(2,1)}, bf16[256,384]{0,1:T(8,128)(2,1)S(1)}, u32[]{:S(2)}, u32[]{:S(2)}) collective-permute-start(bf16[256,384]{0,1:T(8,128)(2,1)} %copy.368), channel_id=1, source_target_pairs={{4,0},{8,4},{12,8},{16,12},{20,16},{24,20},{28,24},{32,28},{36,32}... | collective-permute-start | bytes 589832 | tf_op jit(solution)/shard_map/while/body/eval_jaxpr/ppermute | solution.py:15
  596.5 10.8 %collective-permute-start = (bf16[256,384]{0,1:T(8,128)(2,1)}, bf16[256,384]{0,1:T(8,128)(2,1)S(1)}, u32[]{:S(2)}, u32[]{:S(2)}) collective-permute-start(bf16[256,384]{0,1:T(8,128)(2,1)} %copy.368), channel_id=1, source_target_pairs={{4,0},{8,4},{12,8},{16,12},{20,16},{24,20},{28,24},{32,28},{36,32}... | collective-permute-start | bytes 589832 | tf_op jit(solution)/shard_map/while/body/eval_jaxpr/ppermute | solution.py:15
  608.0 10.8 %collective-permute-start = (bf16[256,384]{0,1:T(8,128)(2,1)}, bf16[256,384]{0,1:T(8,128)(2,1)S(1)}, u32[]{:S(2)}, u32[]{:S(2)}) collective-permute-start(bf16[256,384]{0,1:T(8,128)(2,1)} %copy.368), channel_id=1, source_target_pairs={{4,0},{8,4},{12,8},{16,12},{20,16},{24,20},{28,24},{32,28},{36,32}... | collective-permute-start | bytes 589832 | tf_op jit(solution)/shard_map/while/body/eval_jaxpr/ppermute | solution.py:15
  619.5 10.8 %collective-permute-start = (bf16[256,384]{0,1:T(8,128)(2,1)}, bf16[256,384]{0,1:T(8,128)(2,1)S(1)}, u32[]{:S(2)}, u32[]{:S(2)}) collective-permute-start(bf16[256,384]{0,1:T(8,128)(2,1)} %copy.368), channel_id=1, source_target_pairs={{4,0},{8,4},{12,8},{16,12},{20,16},{24,20},{28,24},{32,28},{36,32}... | collective-permute-start | bytes 589832 | tf_op jit(solution)/shard_map/while/body/eval_jaxpr/ppermute | solution.py:15
  631.0 10.8 %collective-permute-start = (bf16[256,384]{0,1:T(8,128)(2,1)}, bf16[256,384]{0,1:T(8,128)(2,1)S(1)}, u32[]{:S(2)}, u32[]{:S(2)}) collective-permute-start(bf16[256,384]{0,1:T(8,128)(2,1)} %copy.368), channel_id=1, source_target_pairs={{4,0},{8,4},{12,8},{16,12},{20,16},{24,20},{28,24},{32,28},{36,32}... | collective-permute-start | bytes 589832 | tf_op jit(solution)/shard_map/while/body/eval_jaxpr/ppermute | solution.py:15
  642.6 10.8 %collective-permute-start = (bf16[256,384]{0,1:T(8,128)(2,1)}, bf16[256,384]{0,1:T(8,128)(2,1)S(1)}, u32[]{:S(2)}, u32[]{:S(2)}) collective-permute-start(bf16[256,384]{0,1:T(8,128)(2,1)} %copy.368), channel_id=1, source_target_pairs={{4,0},{8,4},{12,8},{16,12},{20,16},{24,20},{28,24},{32,28},{36,32}... | collective-permute-start | bytes 589832 | tf_op jit(solution)/shard_map/while/body/eval_jaxpr/ppermute | solution.py:15
  654.1 10.8 %collective-permute-start = (bf16[256,384]{0,1:T(8,128)(2,1)}, bf16[256,384]{0,1:T(8,128)(2,1)S(1)}, u32[]{:S(2)}, u32[]{:S(2)}) collective-permute-start(bf16[256,384]{0,1:T(8,128)(2,1)} %copy.368), channel_id=1, source_target_pairs={{4,0},{8,4},{12,8},{16,12},{20,16},{24,20},{28,24},{32,28},{36,32}... | collective-permute-start | bytes 589832 | tf_op jit(solution)/shard_map/while/body/eval_jaxpr/ppermute | solution.py:15
  665.6 10.8 %collective-permute-start = (bf16[256,384]{0,1:T(8,128)(2,1)}, bf16[256,384]{0,1:T(8,128)(2,1)S(1)}, u32[]{:S(2)}, u32[]{:S(2)}) collective-permute-start(bf16[256,384]{0,1:T(8,128)(2,1)} %copy.368), channel_id=1, source_target_pairs={{4,0},{8,4},{12,8},{16,12},{20,16},{24,20},{28,24},{32,28},{36,32}... | collective-permute-start | bytes 589832 | tf_op jit(solution)/shard_map/while/body/eval_jaxpr/ppermute | solution.py:15
  677.1 10.8 %collective-permute-start = (bf16[256,384]{0,1:T(8,128)(2,1)}, bf16[256,384]{0,1:T(8,128)(2,1)S(1)}, u32[]{:S(2)}, u32[]{:S(2)}) collective-permute-start(bf16[256,384]{0,1:T(8,128)(2,1)} %copy.368), channel_id=1, source_target_pairs={{4,0},{8,4},{12,8},{16,12},{20,16},{24,20},{28,24},{32,28},{36,32}... | collective-permute-start | bytes 589832 | tf_op jit(solution)/shard_map/while/body/eval_jaxpr/ppermute | solution.py:15
  688.6 10.8 %collective-permute-start = (bf16[256,384]{0,1:T(8,128)(2,1)}, bf16[256,384]{0,1:T(8,128)(2,1)S(1)}, u32[]{:S(2)}, u32[]{:S(2)}) collective-permute-start(bf16[256,384]{0,1:T(8,128)(2,1)} %copy.368), channel_id=1, source_target_pairs={{4,0},{8,4},{12,8},{16,12},{20,16},{24,20},{28,24},{32,28},{36,32}... | collective-permute-start | bytes 589832 | tf_op jit(solution)/shard_map/while/body/eval_jaxpr/ppermute | solution.py:15
  (111 other events, 1240.2 us)
Sparse Core Ops, SparseCore 0:
  12.8 49.5 all-gather.9
  64.5 52.9 all-gather.7
  120.3 45.5 all-gather.11
  168.5 52.8 all-gather.5
where the time goes:
time: 715 us; the launch traced here: 712 us
  starting transfers between devices  184 us (26%)
  local copies, waits for them, and re-layouts  133 us (19%)
  matrix products  126 us (18%)
  waiting for transfers between devices  113 us (16%)
  blocking collectives  81.1 us (11%)
  other arithmetic  33.7 us (5%)
  loops' own time  23.3 us (3%)
  between operations  17.5 us (2%)
    ppermute x124, starting transfers between devices, shifted(): return lax.ppermute(block, axis, route)  184 us
    while x133, local copies, waits for them, and re-layouts  78.9 us
    unnamed x1, blocking collectives  63.9 us
    ppermute x124, waiting for transfers between devices, shifted(): return lax.ppermute(block, axis, route)  50.2 us
    all_gather x1, waiting for transfers between devices, on_device(): lax.all_gather(soft_value, 'seq', axis=0, tiled=True)  46.7 us
    dot_general x9, matrix products, dq_step(): jnp.einsum('htk,khd->thd', dscores, key_part, preferred_element_type=jnp....  24.5 us
    dot_general x15, matrix products, work(): jnp.einsum('htk,thd->khd', dscores, query_part, preferred_element_type=jn...  24.2 us
    dot_general x15, matrix products, work(): jnp.einsum('thd,khd->htk', query_part, own_keys, preferred_element_type=j...  21 us
  transfers between devices with their start and end apart: 128, of which 37 were waited for; matrix products, arithmetic and copies ran while one was open for 26% of the time, Pallas kernels for 0%

commit v1 on v0

--- a/solution.py
+++ b/solution.py
@@ -61,7 +61,9 @@
     block_keys = min(512, seq_count * tok_rows)
     keys_all, values_all = (
         lax.all_gather(soft_key, "seq", axis=0, tiled=True),
-        lax.all_gather(soft_value, "seq", axis=0, tiled=True),
+        jnp.concatenate(
+            lax.all_to_all(jnp.stack([soft_value] * lax.axis_size("seq")), "seq", 0, 0), axis=0
+        ),
     )
     keys_all = jnp.roll(keys_all, group_of[0] * tok_rows, axis=0)
     values_all = jnp.roll(values_all, group_of[0] * tok_rows, axis=0)

time: 715 us -> 796 us (1.11)
  waiting for transfers between devices: 113 us -> 150 us
  starting transfers between devices: 184 us -> 206 us
  local copies, waits for them, and re-layouts: 133 us -> 153 us
    all_to_all x0 -> x1, waiting for transfers between devices: none -> 79.5 us  [on_device(): lax.all_to_all(jnp.stack([soft_value] * lax.axis_size('seq')), 'seq', 0, 0)]
    all_gather x1 -> x0, waiting for transfers between devices: 46.7 us -> none  [on_device(): lax.all_gather(soft_value, 'seq', axis=0, tiled=True)]
    all_gather x1, waiting for transfers between devices: 16.6 us -> 0.01 us  [on_device(): lax.all_gather(shortened(read_grad[None]), 'seq', axis=0, tiled=True)]
    all_gather x1, waiting for transfers between devices: 0.01 us -> 15.8 us  [on_device(): lax.all_gather(soft_key, 'seq', axis=0, tiled=True)]
    all_to_all x0 -> x1, starting transfers between devices: none -> 13.3 us  [on_device(): lax.all_to_all(jnp.stack([soft_value] * lax.axis_size('seq')), 'seq', 0, 0)]
    ppermute x124, starting transfers between devices: 184 us -> 193 us  [shifted(): return lax.ppermute(block, axis, route)]
    all_to_all x0 -> x1, local copies, waits for them, and re-layouts: none -> 8.64 us  [on_device(): lax.all_to_all(jnp.stack([soft_value] * lax.axis_size('seq')), 'seq', 0, 0)]
    unnamed x54 -> x61, local copies, waits for them, and re-layouts: 17.8 us -> 25 us
  transfers between devices with their start and end apart: 128 -> 128, of which waited for: 37 -> 38; matrix products, arithmetic and copies ran while one was open for 26% -> 23% of each run, Pallas kernels for 0% -> 0%
where the time goes in v1:
time: 796 us; the launch traced here: 793 us
  starting transfers between devices  206 us (26%)
  local copies, waits for them, and re-layouts  153 us (19%)
  waiting for transfers between devices  150 us (19%)
  matrix products  127 us (16%)
  blocking collectives  79.9 us (10%)
  other arithmetic  35.1 us (4%)
  loops' own time  23.6 us (3%)
  between operations  17.5 us (2%)
    ppermute x124, starting transfers between devices, shifted(): return lax.ppermute(block, axis, route)  193 us
    all_to_all x1, waiting for transfers between devices, on_device(): lax.all_to_all(jnp.stack([soft_value] * lax.axis_size('seq')), 'seq', 0, 0)  79.5 us
    while x133, local copies, waits for them, and re-layouts  78.7 us
    unnamed x1, blocking collectives  64.1 us
    ppermute x124, waiting for transfers between devices, shifted(): return lax.ppermute(block, axis, route)  54.7 us
    unnamed x61, local copies, waits for them, and re-layouts  25 us
    dot_general x9, matrix products, dq_step(): jnp.einsum('htk,khd->thd', dscores, key_part, preferred_element_type=jnp....  24.4 us
    dot_general x15, matrix products, work(): jnp.einsum('htk,thd->khd', dscores, query_part, preferred_element_type=jn...  24.2 us
  transfers between devices with their start and end apart: 128, of which 38 were waited for; matrix products, arithmetic and copies ran while one was open for 23% of the time, Pallas kernels for 0%

profile of v1, /device:TPU:1, one launch (start us, length us, event | category | flops | bytes accessed | tf_op | source)
XLA Modules:
  0.0 792.7 jit_solution(6004625815793965316)
XLA Ops:
  17.1 64.1 %all-reduce = bf16[96]{0:T(256)(128)(2,1)S(1)} all-reduce(bf16[96]{0:T(256)(128)(2,1)S(1)} %dynamic-update-slice), channel_id=2, replica_groups=mesh['seq'=32,'head'=4] {'seq'}, use_global_device_ids=true, to_apply=%add | all-reduce | flops 96 | bytes 384
  85.4 6.8 fusion.60
  93.4 9.8 %psum.14 = f32[256]{0:T(256)S(1)} all-reduce(f32[256]{0:T(256)S(1)} %get-tuple-element.845), channel_id=1, replica_groups=mesh['seq'=32,'head'=4] {'head'}, use_global_device_ids=true, to_apply=%region_18.20 | all-reduce | flops 256 | bytes 2048 | tf_op jit(solution)/shard_map/psum | solution.py:216
  103.3 6.0 psum.15
  115.9 13.3 %all-to-all-start = ((bf16[32,256,384]{1,2,0:T(8,128)(2,1)}), bf16[32,256,384]{1,2,0:T(8,128)(2,1)}, u32[]{:S(2)}, u32[]{:S(2)}) async-start(bf16[32,256,384]{1,2,0:T(8,128)(2,1)} %stack.2), calls=%async_computation | async-start | bytes 12582912 | tf_op jit(solution)/shard_map/all_to_all | solution.py:65
  136.0 79.5 %all-to-all-done = bf16[32,256,384]{1,2,0:T(8,128)(2,1)} async-done(((bf16[32,256,384]{1,2,0:T(8,128)(2,1)}), bf16[32,256,384]{1,2,0:T(8,128)(2,1)}, u32[]{:S(2)}, u32[]{:S(2)}) %all-to-all-start) | async-done | bytes 6291488 | tf_op jit(solution)/shard_map/all_to_all | solution.py:65
  215.5 8.6 %copy.201 = bf16[32,256,384]{2,1,0:T(8,128)(2,1)} copy(bf16[32,256,384]{1,2,0:T(8,128)(2,1)} %all-to-all-done) | data formatting | bytes 12582912 | tf_op jit(solution)/shard_map/all_to_all | solution.py:65
  224.2 9.2 %fusion.57 = bf16[8192,384]{1,0:T(8,128)(2,1)} fusion(s32[]{:T(128)S(6)} %select_n.73, bf16[8192,384]{1,0:T(8,128)(2,1)} %bitcast.269), kind=kLoop, calls=%fused_computation.87 | loop fusion | flops 12582912 | bytes 12582916 | tf_op jit(solution)/shard_map/jit(_roll_dynamic)/concatenate | solution.py:69
  233.3 8.8 %copy.206 = bf16[8192,384]{0,1:T(8,128)(2,1)} copy(bf16[8192,384]{1,0:T(8,128)(2,1)} %fusion.57) | data formatting | bytes 12582912
  244.8 6.6 fusion.58
  253.7 15.8 %all-gather.5.cloned.1.call-done = bf16[8192,384]{0,1:T(8,128)(2,1)} async-done(((bf16[256,384]{0,1:T(8,128)(2,1)}), bf16[8192,384]{0,1:T(8,128)(2,1)}) %all-gather.5.cloned.1.call-update) | async-done | bytes 6291472 | tf_op jit(solution)/shard_map/all_gather | solution.py:63
  269.5 8.4 %fusion.56 = bf16[8192,384]{0,1:T(8,128)(2,1)} fusion(s32[]{:T(128)S(6)} %select_n.73, bf16[8192,384]{0,1:T(8,128)(2,1)} %all-gather.5.cloned.1.call-done), kind=kLoop, calls=%fused_computation.86 | loop fusion | flops 12582912 | bytes 12582916 | tf_op jit(solution)/shard_map/jit(_roll_dynamic)/concatenate | solution.py:68
  277.9 17.8 %while.60 = (s32[]{:T(128)}, f32[3,256]{1,0:T(4,128)S(1)}, f32[3,256]{1,0:T(4,128)S(1)}, s32[]{:T(128)}, bf16[8192,384]{0,1:T(8,128)(2,1)}, /*index=5*/bf16[256,...) while((s32[]{:T(128)}, f32[3,256]{1,0:T(4,128)S(1)}, ...), condition=%wide.region_3.5_spmd.clone, body=%wide.region_0.4_spmd.clone.sunk | while | flops 102762760 | bytes 4830383 | solution.py:97
  295.8 19.4 %while.61 = (s32[]{:T(128)}, f32[256,3,128]{0,2,1:T(8,128)S(1)}, s32[]{:T(128)}, bf16[8192,384]{0,1:T(8,128)(2,1)}, bf16[8192,384]{0,1:T(8,128)(2,1)}, /*index=5...) while((s32[]{:T(128)}, f32[256,3,128]{0,2,1:T(8,128)S(1)}, ...), condition=%wide.region_5.7_spmd.clone, body=%wide.region_4.6_spmd.clone.sunk | while | flops 203129600 | bytes 3613879 | solution.py:109
  316.9 46.1 %while.62 = (s32[]{:T(128)}, f32[256,3,128]{0,2,1:T(8,128)}, s32[]{:T(128)}, bf16[8192,384]{0,1:T(8,128)(2,1)}, bf16[256,3,128]{2,0,1:T(8,128)(2,1)S(1)}, /*inde...) while((s32[]{:T(128)}, f32[256,3,128]{0,2,1:T(8,128)}, ...), condition=%wide.region_8.10_spmd.clone, body=%wide.region_7.9_spmd.clone.sunk | while | flops 304579328 | bytes 7352519 | solution.py:172
  365.0 414.3 %while.63 = (s32[]{:T(128)}, f32[256,3,128]{2,0,1:T(8,128)S(1)}, f32[256,3,128]{2,0,1:T(8,128)S(1)}, bf16[256,384]{0,1:T(8,128)(2,1)S(1)}, bf16[256,384]{0,1:T(8...) while((s32[]{:T(128)}, f32[256,3,128]{2,0,1:T(8,128)S(1)}, ...), condition=%wide.region_12.14_spmd.clone.clone, body=%wide.region_9.13_spmd.clone.clone.sunk | while | flops 202965248 | bytes 7650759 | solution.py:156
  372.9 8.8 %collective-permute-done.2 = f32[3,256]{1,0:T(4,128)S(1)} collective-permute-done((f32[3,256]{1,0:T(4,128)}, f32[3,256]{1,0:T(4,128)S(1)}, u32[]{:S(2)}, u32[]{:S(2)}) %collective-permute-start.2) | collective-permute-done | bytes 3104 | tf_op jit(solution)/shard_map/while/body/eval_jaxpr/ppermute | solution.py:15
  410.8 64.9 %collective-permute-start.1 = (bf16[256,384]{0,1:T(8,128)(2,1)}, bf16[256,384]{0,1:T(8,128)(2,1)S(1)}, u32[]{:S(2)}, u32[]{:S(2)}) collective-permute-start(bf16[256,384]{0,1:T(8,128)(2,1)} %copy.372), channel_id=1, source_target_pairs={{4,0},{8,4},{12,8},{16,12},{20,16},{24,20},{28,24},{32,28},{36,32}... | collective-permute-start | bytes 589832 | tf_op jit(solution)/shard_map/while/body/eval_jaxpr/ppermute | solution.py:15
  620.1 5.2 collective-permute-start.1
  631.6 5.2 collective-permute-start.1
  643.1 5.2 collective-permute-start.1
  654.6 5.2 collective-permute-start.1
  666.1 5.2 collective-permute-start.1
  677.6 5.2 collective-permute-start.1
  689.1 5.2 collective-permute-start.1
  700.6 5.2 collective-permute-start.1
  712.1 5.2 collective-permute-start.1
  723.6 5.2 collective-permute-start.1
  735.1 5.2 collective-permute-start.1
  746.7 5.2 collective-permute-start.1
  758.2 5.2 collective-permute-start.1
  769.7 5.2 collective-permute-start.1
  (796 shorter events, 436.2 us)
Async XLA Ops:
  7.2 78.2 %all-gather.7.cloned.1.call-start = ((), (), s32[]{:S(2)}) async-start(), calls=%async_computation.2 | async-start | bytes 4325376 | tf_op jit(solution)/shard_map/all_gather | solution.py:202
  12.7 232.1 %all-gather.9.cloned.1.call-start = ((), (), s32[]{:S(2)}) async-start(), calls=%async_computation.3 | async-start | bytes 4325376 | tf_op jit(solution)/shard_map/all_gather | solution.py:236
  110.6 158.9 %all-gather.5.cloned.1.call-start = ((), (), s32[]{:S(2)}) async-start(), calls=%async_computation.1 | async-start | bytes 6488064 | tf_op jit(solution)/shard_map/all_gather | solution.py:63
  115.9 99.6 %all-to-all-start = ((bf16[32,256,384]{1,2,0:T(8,128)(2,1)}), bf16[32,256,384]{1,2,0:T(8,128)(2,1)}, u32[]{:S(2)}, u32[]{:S(2)}) async-start(bf16[32,256,384]{1,2,0:T(8,128)(2,1)} %stack.2), calls=%async_computation | async-start | bytes 12582912 | tf_op jit(solution)/shard_map/all_to_all | solution.py:65
  365.7 16.1 %collective-permute-start = (bf16[256,384]{0,1:T(8,128)(2,1)}, bf16[256,384]{0,1:T(8,128)(2,1)S(1)}, u32[]{:S(2)}, u32[]{:S(2)}) collective-permute-start(bf16[256,384]{0,1:T(8,128)(2,1)} %copy.371), channel_id=1, source_target_pairs={{4,0},{8,4},{12,8},{16,12},{20,16},{24,20},{28,24},{32,28},{36,32}... | collective-permute-start | bytes 589832 | tf_op jit(solution)/shard_map/while/body/eval_jaxpr/ppermute | solution.py:15
  366.6 15.1 %collective-permute-start.1 = (bf16[256,384]{0,1:T(8,128)(2,1)}, bf16[256,384]{0,1:T(8,128)(2,1)S(1)}, u32[]{:S(2)}, u32[]{:S(2)}) collective-permute-start(bf16[256,384]{0,1:T(8,128)(2,1)} %copy.372), channel_id=1, source_target_pairs={{4,0},{8,4},{12,8},{16,12},{20,16},{24,20},{28,24},{32,28},{36,32}... | collective-permute-start | bytes 589832 | tf_op jit(solution)/shard_map/while/body/eval_jaxpr/ppermute | solution.py:15
  367.2 14.5 %collective-permute-start.2 = (f32[3,256]{1,0:T(4,128)}, f32[3,256]{1,0:T(4,128)S(1)}, u32[]{:S(2)}, u32[]{:S(2)}) collective-permute-start(f32[3,256]{1,0:T(4,128)} %copy.373), channel_id=1, source_target_pairs={{4,0},{8,4},{12,8},{16,12},{20,16},{24,20},{28,24},{32,28},{36,32}... | collective-permute-start | bytes 9224 | tf_op jit(solution)/shard_map/while/body/eval_jaxpr/ppermute | solution.py:15
  367.8 13.9 %collective-permute-start.3 = (f32[3,256]{1,0:T(4,128)}, f32[3,256]{1,0:T(4,128)S(1)}, u32[]{:S(2)}, u32[]{:S(2)}) collective-permute-start(f32[3,256]{1,0:T(4,128)} %copy.374), channel_id=1, source_target_pairs={{4,0},{8,4},{12,8},{16,12},{20,16},{24,20},{28,24},{32,28},{36,32}... | collective-permute-start | bytes 9224 | tf_op jit(solution)/shard_map/while/body/eval_jaxpr/ppermute | solution.py:15
  410.1 72.1 %collective-permute-start = (bf16[256,384]{0,1:T(8,128)(2,1)}, bf16[256,384]{0,1:T(8,128)(2,1)S(1)}, u32[]{:S(2)}, u32[]{:S(2)}) collective-permute-start(bf16[256,384]{0,1:T(8,128)(2,1)} %copy.371), channel_id=1, source_target_pairs={{4,0},{8,4},{12,8},{16,12},{20,16},{24,20},{28,24},{32,28},{36,32}... | collective-permute-start | bytes 589832 | tf_op jit(solution)/shard_map/while/body/eval_jaxpr/ppermute | solution.py:15
  410.8 71.4 %collective-permute-start.1 = (bf16[256,384]{0,1:T(8,128)(2,1)}, bf16[256,384]{0,1:T(8,128)(2,1)S(1)}, u32[]{:S(2)}, u32[]{:S(2)}) collective-permute-start(bf16[256,384]{0,1:T(8,128)(2,1)} %copy.372), channel_id=1, source_target_pairs={{4,0},{8,4},{12,8},{16,12},{20,16},{24,20},{28,24},{32,28},{36,32}... | collective-permute-start | bytes 589832 | tf_op jit(solution)/shard_map/while/body/eval_jaxpr/ppermute | solution.py:15
  494.2 10.8 %collective-permute-start = (bf16[256,384]{0,1:T(8,128)(2,1)}, bf16[256,384]{0,1:T(8,128)(2,1)S(1)}, u32[]{:S(2)}, u32[]{:S(2)}) collective-permute-start(bf16[256,384]{0,1:T(8,128)(2,1)} %copy.371), channel_id=1, source_target_pairs={{4,0},{8,4},{12,8},{16,12},{20,16},{24,20},{28,24},{32,28},{36,32}... | collective-permute-start | bytes 589832 | tf_op jit(solution)/shard_map/while/body/eval_jaxpr/ppermute | solution.py:15
  517.2 10.8 %collective-permute-start = (bf16[256,384]{0,1:T(8,128)(2,1)}, bf16[256,384]{0,1:T(8,128)(2,1)S(1)}, u32[]{:S(2)}, u32[]{:S(2)}) collective-permute-start(bf16[256,384]{0,1:T(8,128)(2,1)} %copy.371), channel_id=1, source_target_pairs={{4,0},{8,4},{12,8},{16,12},{20,16},{24,20},{28,24},{32,28},{36,32}... | collective-permute-start | bytes 589832 | tf_op jit(solution)/shard_map/while/body/eval_jaxpr/ppermute | solution.py:15
  528.8 10.8 %collective-permute-start = (bf16[256,384]{0,1:T(8,128)(2,1)}, bf16[256,384]{0,1:T(8,128)(2,1)S(1)}, u32[]{:S(2)}, u32[]{:S(2)}) collective-permute-start(bf16[256,384]{0,1:T(8,128)(2,1)} %copy.371), channel_id=1, source_target_pairs={{4,0},{8,4},{12,8},{16,12},{20,16},{24,20},{28,24},{32,28},{36,32}... | collective-permute-start | bytes 589832 | tf_op jit(solution)/shard_map/while/body/eval_jaxpr/ppermute | solution.py:15
  540.3 10.8 %collective-permute-start = (bf16[256,384]{0,1:T(8,128)(2,1)}, bf16[256,384]{0,1:T(8,128)(2,1)S(1)}, u32[]{:S(2)}, u32[]{:S(2)}) collective-permute-start(bf16[256,384]{0,1:T(8,128)(2,1)} %copy.371), channel_id=1, source_target_pairs={{4,0},{8,4},{12,8},{16,12},{20,16},{24,20},{28,24},{32,28},{36,32}... | collective-permute-start | bytes 589832 | tf_op jit(solution)/shard_map/while/body/eval_jaxpr/ppermute | solution.py:15
  551.8 10.8 %collective-permute-start = (bf16[256,384]{0,1:T(8,128)(2,1)}, bf16[256,384]{0,1:T(8,128)(2,1)S(1)}, u32[]{:S(2)}, u32[]{:S(2)}) collective-permute-start(bf16[256,384]{0,1:T(8,128)(2,1)} %copy.371), channel_id=1, source_target_pairs={{4,0},{8,4},{12,8},{16,12},{20,16},{24,20},{28,24},{32,28},{36,32}... | collective-permute-start | bytes 589832 | tf_op jit(solution)/shard_map/while/body/eval_jaxpr/ppermute | solution.py:15
  574.8 10.8 %collective-permute-start = (bf16[256,384]{0,1:T(8,128)(2,1)}, bf16[256,384]{0,1:T(8,128)(2,1)S(1)}, u32[]{:S(2)}, u32[]{:S(2)}) collective-permute-start(bf16[256,384]{0,1:T(8,128)(2,1)} %copy.371), channel_id=1, source_target_pairs={{4,0},{8,4},{12,8},{16,12},{20,16},{24,20},{28,24},{32,28},{36,32}... | collective-permute-start | bytes 589832 | tf_op jit(solution)/shard_map/while/body/eval_jaxpr/ppermute | solution.py:15
  586.3 10.8 %collective-permute-start = (bf16[256,384]{0,1:T(8,128)(2,1)}, bf16[256,384]{0,1:T(8,128)(2,1)S(1)}, u32[]{:S(2)}, u32[]{:S(2)}) collective-permute-start(bf16[256,384]{0,1:T(8,128)(2,1)} %copy.371), channel_id=1, source_target_pairs={{4,0},{8,4},{12,8},{16,12},{20,16},{24,20},{28,24},{32,28},{36,32}... | collective-permute-start | bytes 589832 | tf_op jit(solution)/shard_map/while/body/eval_jaxpr/ppermute | solution.py:15
  607.4 10.8 %collective-permute-start = (bf16[256,384]{0,1:T(8,128)(2,1)}, bf16[256,384]{0,1:T(8,128)(2,1)S(1)}, u32[]{:S(2)}, u32[]{:S(2)}) collective-permute-start(bf16[256,384]{0,1:T(8,128)(2,1)} %copy.371), channel_id=1, source_target_pairs={{4,0},{8,4},{12,8},{16,12},{20,16},{24,20},{28,24},{32,28},{36,32}... | collective-permute-start | bytes 589832 | tf_op jit(solution)/shard_map/while/body/eval_jaxpr/ppermute | solution.py:15
  618.9 10.8 %collective-permute-start = (bf16[256,384]{0,1:T(8,128)(2,1)}, bf16[256,384]{0,1:T(8,128)(2,1)S(1)}, u32[]{:S(2)}, u32[]{:S(2)}) collective-permute-start(bf16[256,384]{0,1:T(8,128)(2,1)} %copy.371), channel_id=1, source_target_pairs={{4,0},{8,4},{12,8},{16,12},{20,16},{24,20},{28,24},{32,28},{36,32}... | collective-permute-start | bytes 589832 | tf_op jit(solution)/shard_map/while/body/eval_jaxpr/ppermute | solution.py:15
  630.4 10.8 %collective-permute-start = (bf16[256,384]{0,1:T(8,128)(2,1)}, bf16[256,384]{0,1:T(8,128)(2,1)S(1)}, u32[]{:S(2)}, u32[]{:S(2)}) collective-permute-start(bf16[256,384]{0,1:T(8,128)(2,1)} %copy.371), channel_id=1, source_target_pairs={{4,0},{8,4},{12,8},{16,12},{20,16},{24,20},{28,24},{32,28},{36,32}... | collective-permute-start | bytes 589832 | tf_op jit(solution)/shard_map/while/body/eval_jaxpr/ppermute | solution.py:15
  641.9 10.8 %collective-permute-start = (bf16[256,384]{0,1:T(8,128)(2,1)}, bf16[256,384]{0,1:T(8,128)(2,1)S(1)}, u32[]{:S(2)}, u32[]{:S(2)}) collective-permute-start(bf16[256,384]{0,1:T(8,128)(2,1)} %copy.371), channel_id=1, source_target_pairs={{4,0},{8,4},{12,8},{16,12},{20,16},{24,20},{28,24},{32,28},{36,32}... | collective-permute-start | bytes 589832 | tf_op jit(solution)/shard_map/while/body/eval_jaxpr/ppermute | solution.py:15
  653.4 10.8 %collective-permute-start = (bf16[256,384]{0,1:T(8,128)(2,1)}, bf16[256,384]{0,1:T(8,128)(2,1)S(1)}, u32[]{:S(2)}, u32[]{:S(2)}) collective-permute-start(bf16[256,384]{0,1:T(8,128)(2,1)} %copy.371), channel_id=1, source_target_pairs={{4,0},{8,4},{12,8},{16,12},{20,16},{24,20},{28,24},{32,28},{36,32}... | collective-permute-start | bytes 589832 | tf_op jit(solution)/shard_map/while/body/eval_jaxpr/ppermute | solution.py:15
  664.9 10.8 %collective-permute-start = (bf16[256,384]{0,1:T(8,128)(2,1)}, bf16[256,384]{0,1:T(8,128)(2,1)S(1)}, u32[]{:S(2)}, u32[]{:S(2)}) collective-permute-start(bf16[256,384]{0,1:T(8,128)(2,1)} %copy.371), channel_id=1, source_target_pairs={{4,0},{8,4},{12,8},{16,12},{20,16},{24,20},{28,24},{32,28},{36,32}... | collective-permute-start | bytes 589832 | tf_op jit(solution)/shard_map/while/body/eval_jaxpr/ppermute | solution.py:15
  676.4 10.8 %collective-permute-start = (bf16[256,384]{0,1:T(8,128)(2,1)}, bf16[256,384]{0,1:T(8,128)(2,1)S(1)}, u32[]{:S(2)}, u32[]{:S(2)}) collective-permute-start(bf16[256,384]{0,1:T(8,128)(2,1)} %copy.371), channel_id=1, source_target_pairs={{4,0},{8,4},{12,8},{16,12},{20,16},{24,20},{28,24},{32,28},{36,32}... | collective-permute-start | bytes 589832 | tf_op jit(solution)/shard_map/while/body/eval_jaxpr/ppermute | solution.py:15
  687.9 10.8 %collective-permute-start = (bf16[256,384]{0,1:T(8,128)(2,1)}, bf16[256,384]{0,1:T(8,128)(2,1)S(1)}, u32[]{:S(2)}, u32[]{:S(2)}) collective-permute-start(bf16[256,384]{0,1:T(8,128)(2,1)} %copy.371), channel_id=1, source_target_pairs={{4,0},{8,4},{12,8},{16,12},{20,16},{24,20},{28,24},{32,28},{36,32}... | collective-permute-start | bytes 589832 | tf_op jit(solution)/shard_map/while/body/eval_jaxpr/ppermute | solution.py:15
  699.4 10.8 %collective-permute-start = (bf16[256,384]{0,1:T(8,128)(2,1)}, bf16[256,384]{0,1:T(8,128)(2,1)S(1)}, u32[]{:S(2)}, u32[]{:S(2)}) collective-permute-start(bf16[256,384]{0,1:T(8,128)(2,1)} %copy.371), channel_id=1, source_target_pairs={{4,0},{8,4},{12,8},{16,12},{20,16},{24,20},{28,24},{32,28},{36,32}... | collective-permute-start | bytes 589832 | tf_op jit(solution)/shard_map/while/body/eval_jaxpr/ppermute | solution.py:15
  710.9 10.8 %collective-permute-start = (bf16[256,384]{0,1:T(8,128)(2,1)}, bf16[256,384]{0,1:T(8,128)(2,1)S(1)}, u32[]{:S(2)}, u32[]{:S(2)}) collective-permute-start(bf16[256,384]{0,1:T(8,128)(2,1)} %copy.371), channel_id=1, source_target_pairs={{4,0},{8,4},{12,8},{16,12},{20,16},{24,20},{28,24},{32,28},{36,32}... | collective-permute-start | bytes 589832 | tf_op jit(solution)/shard_map/while/body/eval_jaxpr/ppermute | solution.py:15
  722.4 10.8 %collective-permute-start = (bf16[256,384]{0,1:T(8,128)(2,1)}, bf16[256,384]{0,1:T(8,128)(2,1)S(1)}, u32[]{:S(2)}, u32[]{:S(2)}) collective-permute-start(bf16[256,384]{0,1:T(8,128)(2,1)} %copy.371), channel_id=1, source_target_pairs={{4,0},{8,4},{12,8},{16,12},{20,16},{24,20},{28,24},{32,28},{36,32}... | collective-permute-start | bytes 589832 | tf_op jit(solution)/shard_map/while/body/eval_jaxpr/ppermute | solution.py:15
  733.9 10.8 %collective-permute-start = (bf16[256,384]{0,1:T(8,128)(2,1)}, bf16[256,384]{0,1:T(8,128)(2,1)S(1)}, u32[]{:S(2)}, u32[]{:S(2)}) collective-permute-start(bf16[256,384]{0,1:T(8,128)(2,1)} %copy.371), channel_id=1, source_target_pairs={{4,0},{8,4},{12,8},{16,12},{20,16},{24,20},{28,24},{32,28},{36,32}... | collective-permute-start | bytes 589832 | tf_op jit(solution)/shard_map/while/body/eval_jaxpr/ppermute | solution.py:15
  745.5 10.8 %collective-permute-start = (bf16[256,384]{0,1:T(8,128)(2,1)}, bf16[256,384]{0,1:T(8,128)(2,1)S(1)}, u32[]{:S(2)}, u32[]{:S(2)}) collective-permute-start(bf16[256,384]{0,1:T(8,128)(2,1)} %copy.371), channel_id=1, source_target_pairs={{4,0},{8,4},{12,8},{16,12},{20,16},{24,20},{28,24},{32,28},{36,32}... | collective-permute-start | bytes 589832 | tf_op jit(solution)/shard_map/while/body/eval_jaxpr/ppermute | solution.py:15
  757.0 10.8 %collective-permute-start = (bf16[256,384]{0,1:T(8,128)(2,1)}, bf16[256,384]{0,1:T(8,128)(2,1)S(1)}, u32[]{:S(2)}, u32[]{:S(2)}) collective-permute-start(bf16[256,384]{0,1:T(8,128)(2,1)} %copy.371), channel_id=1, source_target_pairs={{4,0},{8,4},{12,8},{16,12},{20,16},{24,20},{28,24},{32,28},{36,32}... | collective-permute-start | bytes 589832 | tf_op jit(solution)/shard_map/while/body/eval_jaxpr/ppermute | solution.py:15
  768.5 10.8 %collective-permute-start = (bf16[256,384]{0,1:T(8,128)(2,1)}, bf16[256,384]{0,1:T(8,128)(2,1)S(1)}, u32[]{:S(2)}, u32[]{:S(2)}) collective-permute-start(bf16[256,384]{0,1:T(8,128)(2,1)} %copy.371), channel_id=1, source_target_pairs={{4,0},{8,4},{12,8},{16,12},{20,16},{24,20},{28,24},{32,28},{36,32}... | collective-permute-start | bytes 589832 | tf_op jit(solution)/shard_map/while/body/eval_jaxpr/ppermute | solution.py:15
  (114 other events, 1704.9 us)
Sparse Core Ops, SparseCore 0:
  12.8 49.5 all-gather.6
  110.8 98.9 all-gather.8
  212.5 57.0 all-gather.4
